TPU v7x, 32 devices: a whole 2x2x4 slice. The times are simulated.
32 devices in a mesh: grp: 8 (over y, x, core), seq: 4 (over z).
Axes of the slice: x: 2, y: 2, z: 4, core: 2. Of those that a mesh axis runs over, the one named last changes fastest.
Arguments:
- tokens: bfloat16 [8192, 2048], P(('grp', 'seq')), may hold values from -6 to 6
- cotangent: bfloat16 [8192, 2048], P(('grp', 'seq')), may hold values from -6 to 6
- segment_ids: int32 [8192], P(('grp', 'seq')), may hold values from 0 to 31, never falling along the last dimension, each value on 1 to 768 neighbouring positions
- tile_owner_slots: int32 [166], replicated, may hold values from 0 to 167, as said below
- weights_low: bfloat16 [168, 2048, 128], P('grp', 'seq')
- master: float32 [168, 2048, 128], P('grp', 'seq')
- moment_one: float32 [168, 2048, 128], P('grp', 'seq')
- moment_two: float32 [168, 2048, 128], P('grp', 'seq'), as said below
- left_basis_set: float32 [168, 2048, 512], P('grp', 'seq'), as said below
- right_basis_set: float32 [168, 512, 128], P('grp', 'seq'), as said below
- gains: float32 [2, 2048], replicated, may hold values from 0.5 to 1.5
- gain_moment_one: float32 [2, 2048], replicated, may hold values from -28 to 28
- gain_moment_two: float32 [2, 2048], replicated, may hold values from 430.8992 to 1720.32
Outputs:
- block_out: bfloat16 [8192, 2048], P(('grp', 'seq'))
- input_grad: float32 [8192, 2048], P(('grp', 'seq'))
- new_master: float32 [168, 2048, 128], P('grp', 'seq')
- new_moment_one: float32 [168, 2048, 128], P('grp', 'seq')
- new_moment_two: float32 [168, 2048, 128], P('grp', 'seq')
- gain_grads: float32 [2, 2048], replicated
- new_gains: float32 [2, 2048], replicated
- new_gain_one: float32 [2, 2048], replicated
- new_gain_two: float32 [2, 2048], replicated
Inputs may be any that keep to these rules, and one draw needn't show every extreme that they name: `tile_owner_slots`: the entries are distinct; slot q belongs to data group q // 21. `segment_ids`: never falls along the tokens. `left_basis_set`: each 512 x 512 block is orthogonal. `right_basis_set`: each 128 x 128 block is orthogonal. `moment_two`: positive.
All inputs are finite; a program needn't handle non-finite values.
Results may differ from a plain program's by a relative error of at most 0.015.
Values may be sent and summed in bfloat16 or wider, within the bound.
A program may use at most 704 MiB of HBM per device.

v0:
```python
import jax
import jax.numpy as jnp
from jax import lax
from jax.sharding import PartitionSpec as P

MODEL_WIDTH = 2048
NH = 16
HD = 128
FF = 5632
SEQLEN = 1024
NORM_EPS = 1e-05
BETA_ONE = 0.95
BETA_TWO = 0.95
ADAM_EPS = 1e-08
WEIGHT_DECAY = 0.01
LEARN_RATE = 0.03
GAIN_RATE = 1.5
ROPE_BASE = 10000.0
MASKED = -1e30
PRECISE = lax.Precision.HIGHEST


def rotate(values, positions, direction):
    head_width = values.shape[-1]
    half_width = head_width // 2
    frequency = ROPE_BASE ** (-(jnp.arange(half_width, dtype=jnp.float32) * 2.0) / head_width)
    angles = positions.astype(jnp.float32)[:, None] * frequency[None, :]
    cosine = jnp.cos(angles)[:, None, :]
    sine_part = (jnp.sin(angles) * direction)[:, None, :]
    leading = values[..., :half_width]
    trailing = values[..., half_width:]
    return jnp.concatenate(
        [leading * cosine - trailing * sine_part, trailing * cosine + leading * sine_part], axis=-1
    )


def visible(query_index, key_index, query_seg, key_seg):
    causal = query_index[:, None] >= key_index[None, :]
    same_seq = query_index[:, None] // SEQLEN == key_index[None, :] // SEQLEN
    same_doc = query_seg[:, None] == key_seg[None, :]
    return causal & same_seq & same_doc


def contract(left_side, right_side):
    return lax.dot_general(
        left_side, right_side, (((0,), (0,)), ((), ())), preferred_element_type=jnp.float32
    )


def times_transpose(left_side, right_side):
    return lax.dot_general(
        left_side, right_side, (((1,), (1,)), ((), ())), preferred_element_type=jnp.float32
    )


def attend(queries, key_rows, value_rows, query_index, query_seg, key_index, key_seg):
    query_total, head_count, head_width = queries.shape
    block_rows = min(512, query_total)
    block_count = query_total // block_rows
    score_scale = head_width ** (-0.5)

    def one_block(inputs):
        block_queries, block_index, block_seg = inputs
        raw_scores = jnp.einsum(
            "qhd,kd->hqk", block_queries, key_rows, preferred_element_type=jnp.float32
        )
        allowed = visible(block_index, key_index, block_seg, key_seg)
        score_matrix = jnp.where(allowed[None], raw_scores * score_scale, MASKED)
        highest = jnp.max(score_matrix, axis=-1, keepdims=True)
        exponent = jnp.exp(score_matrix - highest)
        totals = jnp.sum(exponent, axis=-1, keepdims=True)
        probs_low = (exponent / totals).astype(jnp.bfloat16)
        context = jnp.einsum(
            "hqk,kd->qhd", probs_low, value_rows, preferred_element_type=jnp.float32
        )
        return (context, jnp.transpose((highest + jnp.log(totals))[..., 0]))

    context, log_totals = lax.map(
        one_block,
        (
            queries.reshape(block_count, block_rows, head_count, head_width),
            query_index.reshape(block_count, block_rows),
            query_seg.reshape(block_count, block_rows),
        ),
    )
    return (
        context.reshape(query_total, head_count, head_width),
        log_totals.reshape(query_total, head_count),
    )


def attend_back(
    queries, key_rows, value_rows, grads_low, log_totals, query_index, query_seg, key_index, key_seg
):
    query_total, head_count, head_width = queries.shape
    block_rows = min(512, query_total)
    block_count = query_total // block_rows
    score_scale = head_width ** (-0.5)

    def one_block(running, inputs):
        block_queries, block_grads, block_totals, block_index, block_seg = inputs
        raw_scores = jnp.einsum(
            "qhd,kd->hqk", block_queries, key_rows, preferred_element_type=jnp.float32
        )
        allowed = visible(block_index, key_index, block_seg, key_seg)
        shifted = raw_scores * score_scale - jnp.transpose(block_totals)[:, :, None]
        probs = jnp.where(allowed[None], jnp.exp(shifted), 0.0)
        prob_grad = jnp.einsum(
            "qhd,kd->hqk", block_grads, value_rows, preferred_element_type=jnp.float32
        )
        centre = jnp.sum(probs * prob_grad, axis=-1, keepdims=True)
        score_grad = (probs * (prob_grad - centre) * score_scale).astype(jnp.bfloat16)
        query_part = jnp.einsum(
            "hqk,kd->qhd", score_grad, key_rows, preferred_element_type=jnp.float32
        )
        key_part = running[0] + jnp.einsum(
            "hqk,qhd->kd", score_grad, block_queries, preferred_element_type=jnp.float32
        )
        value_part = running[1] + jnp.einsum(
            "hqk,qhd->kd",
            probs.astype(jnp.bfloat16),
            block_grads,
            preferred_element_type=jnp.float32,
        )
        return ((key_part, value_part), query_part)

    zeros_rows = jnp.zeros(key_rows.shape, jnp.float32)
    (key_grad, value_grad), query_grad = lax.scan(
        one_block,
        (zeros_rows, zeros_rows),
        (
            queries.reshape(block_count, block_rows, head_count, head_width),
            grads_low.reshape(block_count, block_rows, head_count, head_width),
            log_totals.reshape(block_count, block_rows, head_count),
            query_index.reshape(block_count, block_rows),
            query_seg.reshape(block_count, block_rows),
        ),
    )
    return (query_grad.reshape(query_total, head_count, head_width), key_grad, value_grad)


def local(
    tokens,
    cotangent,
    segment_ids,
    tile_owner_slots,
    weights_low,
    master,
    moment_one,
    moment_two,
    left_basis_set,
    right_basis_set,
    gains,
    gain_moment_one,
    gain_moment_two,
):
    grp_count = lax.axis_size("grp")
    seq_count = lax.axis_size("seq")
    grp_here = lax.axis_index("grp")
    rows_here = tokens.shape[0]
    slots_here, rows_block, tile_width = weights_low.shape
    query_cols = NH * HD
    value_end = query_cols + 2 * HD
    output_end = value_end + MODEL_WIDTH
    attn_tiles = output_end // tile_width
    hidden_tiles = FF // tile_width
    share = -(-hidden_tiles // grp_count)
    share_cols = share * tile_width
    sub_rows = rows_block // grp_count
    local_index = lax.axis_index("seq") * rows_here + jnp.arange(rows_here, dtype=jnp.int32)
    local_place = local_index % SEQLEN
    plane_tiles = lax.all_gather(weights_low, "grp", axis=0, tiled=True)
    hidden_ids = grp_here * share + jnp.arange(share, dtype=jnp.int32)
    real = hidden_ids < hidden_tiles
    hidden_ids = jnp.minimum(hidden_ids, hidden_tiles - 1)
    feed_ids = (
        attn_tiles + jnp.arange(3, dtype=jnp.int32)[:, None] * hidden_tiles + hidden_ids[None, :]
    ).reshape(-1)
    attn_rows = lax.dynamic_slice_in_dim(plane_tiles, grp_here * sub_rows, sub_rows, axis=1)
    attn_rows = jnp.transpose(attn_rows[tile_owner_slots[:attn_tiles]], (1, 0, 2)).reshape(
        sub_rows, output_end
    )
    attn_weights = lax.all_gather(attn_rows, "seq", axis=0, tiled=False)
    attn_weights = lax.all_gather(attn_weights, "grp", axis=1, tiled=True).reshape(
        MODEL_WIDTH, output_end
    )
    feed_tiles = jnp.where(
        jnp.tile(real, 3)[:, None, None], plane_tiles[tile_owner_slots[feed_ids]], 0
    )
    feed_rows = jnp.transpose(feed_tiles, (1, 0, 2)).reshape(rows_block, 3 * share_cols)
    feed_weights = lax.all_gather(feed_rows, "seq", axis=0, tiled=True)
    cot_plane = lax.all_gather(cotangent, "grp", axis=0, tiled=True)
    tok_float = tokens.astype(jnp.float32)
    inverse_one = lax.rsqrt(jnp.mean(tok_float * tok_float, axis=-1, keepdims=True) + NORM_EPS)
    normed = (tok_float * inverse_one * gains[0]).astype(jnp.bfloat16)
    projected = jnp.dot(normed, attn_weights[:, :value_end], preferred_element_type=jnp.float32)
    queries = rotate(projected[:, :query_cols].reshape(rows_here, NH, HD), local_place, 1.0).astype(
        jnp.bfloat16
    )
    key_rows = (
        rotate(
            projected[:, query_cols : query_cols + HD].reshape(rows_here, 1, HD), local_place, 1.0
        )
        .reshape(rows_here, HD)
        .astype(jnp.bfloat16)
    )
    value_rows = projected[:, query_cols + HD : value_end].astype(jnp.bfloat16)
    all_pairs = lax.all_gather(
        jnp.concatenate([key_rows, value_rows], axis=1), "seq", axis=0, tiled=True
    )
    all_keys = all_pairs[:, :HD]
    all_values = all_pairs[:, HD:]
    all_segs = lax.all_gather(segment_ids, "seq", axis=0, tiled=True)
    group_index = jnp.arange(all_keys.shape[0], dtype=jnp.int32)
    group_place = group_index % SEQLEN
    heads_here = NH // seq_count
    head_queries = lax.all_to_all(
        queries.reshape(rows_here, query_cols), "seq", split_axis=1, concat_axis=0, tiled=True
    ).reshape(-1, heads_here, HD)
    head_context, log_totals = attend(
        head_queries, all_keys, all_values, group_index, all_segs, group_index, all_segs
    )
    context = lax.all_to_all(
        head_context.reshape(-1, heads_here * HD).astype(jnp.bfloat16),
        "seq",
        split_axis=0,
        concat_axis=1,
        tiled=True,
    )
    branch = jnp.dot(context, attn_weights[:, value_end:], preferred_element_type=jnp.float32)
    hidden = tok_float + branch
    inverse_two = lax.rsqrt(jnp.mean(hidden * hidden, axis=-1, keepdims=True) + NORM_EPS)
    normed_two = (hidden * inverse_two * gains[1]).astype(jnp.bfloat16)
    normed_plane = lax.all_gather(normed_two, "grp", axis=0, tiled=True)
    gating_weights = feed_weights[:, : 2 * share_cols]
    down_weights = feed_weights[:, 2 * share_cols :]
    gate_up = jnp.dot(normed_plane, gating_weights, preferred_element_type=jnp.float32)
    gate = gate_up[:, :share_cols]
    upper = gate_up[:, share_cols:]
    sigmoid_gate = jax.nn.sigmoid(gate)
    silu_gate = jax.nn.silu(gate)
    activated = (silu_gate * upper).astype(jnp.bfloat16)
    act_grad = jnp.dot(cot_plane, down_weights, preferred_element_type=jnp.float32)
    gate_grad = (act_grad * upper * sigmoid_gate * (1.0 + gate * (1.0 - sigmoid_gate))).astype(
        jnp.bfloat16
    )
    up_grad = (act_grad * silu_gate).astype(jnp.bfloat16)
    gating_grad = jnp.concatenate([gate_grad, up_grad], axis=1)
    norm_two_grad = lax.psum_scatter(
        times_transpose(gating_grad, gating_weights).astype(jnp.bfloat16),
        "grp",
        scatter_dimension=0,
        tiled=True,
    ).astype(jnp.float32)
    feed_grads = jnp.concatenate(
        [contract(normed_plane, gating_grad), contract(cot_plane, activated)], axis=1
    ).astype(jnp.bfloat16)
    feed_grads = lax.psum_scatter(feed_grads, "seq", scatter_dimension=0, tiled=True)
    feed_grads = jnp.transpose(feed_grads.reshape(rows_block, 3 * share, tile_width), (1, 0, 2))
    feed_grads = lax.all_gather(feed_grads, "grp", axis=0, tiled=True)
    feed_out = lax.psum_scatter(
        times_transpose(activated, down_weights).astype(jnp.bfloat16),
        "grp",
        scatter_dimension=0,
        tiled=True,
    ).astype(jnp.float32)
    block_out = (hidden + feed_out).astype(jnp.bfloat16)
    out_grad = cotangent.astype(jnp.float32)
    gain_two_term = jnp.sum(norm_two_grad * hidden * inverse_two, axis=0)
    hidden_grad = (
        out_grad
        + inverse_two * gains[1] * norm_two_grad
        - hidden
        * inverse_two**3
        * jnp.mean(hidden * gains[1] * norm_two_grad, axis=-1, keepdims=True)
    )
    branch_grad = hidden_grad.astype(jnp.bfloat16)
    context_grad = times_transpose(branch_grad, attn_weights[:, value_end:]).astype(jnp.bfloat16)
    head_grads = lax.all_to_all(
        context_grad, "seq", split_axis=1, concat_axis=0, tiled=True
    ).reshape(-1, heads_here, HD)

    def reduce_rows(part):
        cols = part.shape[1]
        blocks = jnp.transpose(
            part.astype(jnp.bfloat16).reshape(seq_count, grp_count, sub_rows, cols), (1, 0, 2, 3)
        ).reshape(grp_count * seq_count * sub_rows, cols)
        summed = lax.psum_scatter(blocks, ("grp", "seq"), scatter_dimension=0, tiled=True)
        return lax.all_gather(summed, "grp", axis=0, tiled=True)

    out_grads = reduce_rows(contract(context, branch_grad))
    head_query_grad, key_part, value_part = attend_back(
        head_queries,
        all_keys,
        all_values,
        head_grads,
        log_totals,
        group_index,
        all_segs,
        group_index,
        all_segs,
    )
    turned_query = (
        rotate(head_query_grad, group_place, -1.0).reshape(-1, heads_here * HD).astype(jnp.bfloat16)
    )
    query_grad = lax.all_to_all(turned_query, "seq", split_axis=0, concat_axis=1, tiled=True)
    key_part = rotate(key_part[:, None, :], group_place, -1.0)[:, 0, :]
    pair_grad = lax.psum_scatter(
        jnp.concatenate([key_part, value_part], axis=1), "seq", scatter_dimension=0, tiled=True
    )
    projected_grad = jnp.concatenate([query_grad, pair_grad.astype(jnp.bfloat16)], axis=1)
    in_grads = reduce_rows(contract(normed, projected_grad))
    norm_one_grad = times_transpose(projected_grad, attn_weights[:, :value_end])
    gain_one_term = jnp.sum(norm_one_grad * tok_float * inverse_one, axis=0)
    input_grad = (
        hidden_grad
        + inverse_one * gains[0] * norm_one_grad
        - tok_float
        * inverse_one**3
        * jnp.mean(tok_float * gains[0] * norm_one_grad, axis=-1, keepdims=True)
    )
    gain_grads = lax.psum(jnp.stack([gain_one_term, gain_two_term]), ("grp", "seq"))
    tile_count = tile_owner_slots.shape[0]
    tile_of_slot = (
        jnp.full((grp_count * slots_here,), tile_count, jnp.int32)
        .at[tile_owner_slots]
        .set(jnp.arange(tile_count, dtype=jnp.int32))
    )
    tiles_here = lax.dynamic_slice_in_dim(tile_of_slot, grp_here * slots_here, slots_here)
    attn_grads = jnp.transpose(
        jnp.concatenate([in_grads, out_grads], axis=1).reshape(rows_block, attn_tiles, tile_width),
        (1, 0, 2),
    )
    feed_at = jnp.clip(tiles_here - attn_tiles, 0, 3 * hidden_tiles - 1)
    which, column = (feed_at // hidden_tiles, feed_at % hidden_tiles)
    feed_at = column // share * (3 * share) + which * share + column % share
    picked = jnp.where(
        (tiles_here < attn_tiles)[:, None, None],
        attn_grads[jnp.minimum(tiles_here, attn_tiles - 1)],
        feed_grads[feed_at],
    )
    reduced_sum = jnp.where((tiles_here < tile_count)[:, None, None], picked, 0).astype(jnp.float32)
    turned = jnp.einsum("zji,zjc->zic", left_basis_set, reduced_sum)
    turned = jnp.einsum("zic,zcd->zid", turned, right_basis_set)
    new_one = BETA_ONE * moment_one + (1.0 - BETA_ONE) * turned
    new_two = BETA_TWO * moment_two + (1.0 - BETA_TWO) * turned * turned
    scaled = new_one / (jnp.sqrt(new_two) + ADAM_EPS)
    restored = jnp.einsum("zij,zjd->zid", left_basis_set, scaled)
    restored = jnp.einsum("zid,zed->zie", restored, right_basis_set)
    new_master = master * (1.0 - LEARN_RATE * WEIGHT_DECAY) - LEARN_RATE * restored
    gain_one = BETA_ONE * gain_moment_one + (1.0 - BETA_ONE) * gain_grads
    gain_two = BETA_TWO * gain_moment_two + (1.0 - BETA_TWO) * gain_grads * gain_grads
    new_gains = gains - GAIN_RATE * gain_one / (jnp.sqrt(gain_two) + ADAM_EPS)
    return (
        block_out,
        input_grad,
        new_master,
        new_one,
        new_two,
        gain_grads,
        new_gains,
        gain_one,
        gain_two,
    )


def solution(mesh):
    return jax.shard_map(
        local,
        mesh=mesh,
        in_specs=(
            P(("grp", "seq"), None),
            P(("grp", "seq"), None),
            P(("grp", "seq")),
            P(),
            P("grp", "seq", None),
            P("grp", "seq", None),
            P("grp", "seq", None),
            P("grp", "seq", None),
            P("grp", "seq", None),
            P("grp", "seq", None),
            P(),
            P(),
            P(),
        ),
        out_specs=(
            P(("grp", "seq"), None),
            P(("grp", "seq"), None),
            P("grp", "seq", None),
            P("grp", "seq", None),
            P("grp", "seq", None),
            P(),
            P(),
            P(),
            P(),
        ),
        check_vma=False,
    )
```

profile of v0, /device:TPU:0, one launch (start us, length us, event | category | flops | bytes accessed | tf_op | source)
XLA Modules:
  0.0 1731.6 jit_solution(6610942294189539147)
XLA Ops:
  8.7 116.0 %all-gather.11.cloned.1.call-done = bf16[168,512,128]{2,1,0:T(8,128)(2,1)} async-done(((bf16[21,512,128]{2,1,0:T(8,128)(2,1)}), bf16[168,512,128]{2,1,0:T(8,128)(2,1)}) %all-gather.11.cloned.1.call-update) | async-done | bytes 22020112 | tf_op jit(solution)/shard_map/all_gather | solution.py:172
  134.4 48.4 %all-gather.13.cloned.1.call-done = bf16[4,64,4352]{2,1,0:T(8,128)(2,1)} async-done(((bf16[1,64,4352]{2,1,0:T(8,128)(2,1)}), bf16[4,64,4352]{2,1,0:T(8,128)(2,1)}) %all-gather.13.cloned.1.call-update) | async-done | bytes 2228240 | tf_op jit(solution)/shard_map/all_gather | solution.py:183
  204.3 73.6 %all-gather.15.cloned.1.call-done = bf16[4,512,4352]{2,1,0:T(8,128)(2,1)} async-done(((bf16[4,64,4352]{2,1,0:T(8,128)(2,1)}), bf16[4,512,4352]{2,1,0:T(8,128)(2,1)}) %all-gather.15.cloned.1.call-update) | async-done | bytes 17825808 | tf_op jit(solution)/shard_map/all_gather | solution.py:184
  296.3 40.8 %all-gather = s32[4,1,256]{2,1,0:T(1,128)S(1)} all-gather(s32[1,1,256]{2,1,0:T(1,128)} %bitcast.336), channel_id=1, replica_groups=mesh['grp'=8,'seq'=4] {'seq'}, dimensions={0}, use_global_device_ids=true | all-gather | bytes 5120 | tf_op jit(solution)/shard_map/all_gather | solution.py:213
  339.6 43.2 %all_gather.37 = bf16[1024,256]{0,1:T(8,128)(2,1)S(1)} all-gather(bf16[256,256]{0,1:T(8,128)(2,1)S(1)} %pad_maximum_fusion.11), channel_id=1, replica_groups=mesh['grp'=8,'seq'=4] {'seq'}, dimensions={0}, use_global_device_ids=true | all-gather | bytes 655360 | tf_op jit(solution)/shard_map/all_gather | solution.py:208
  410.6 59.3 %all_to_all.61 = bf16[4,256,512]{2,1,0:T(8,128)(2,1)} all-to-all(bf16[4,256,512]{2,1,0:T(8,128)(2,1)} %convert_element_type.137), channel_id=1, replica_groups=mesh['grp'=8,'seq'=4] {'seq'}, dimensions={0} | all-to-all | bytes 2097152 | tf_op jit(solution)/shard_map/all_to_all | solution.py:223
  499.8 54.9 %all-gather.17.cloned.1.call-done = bf16[2048,2048]{1,0:T(8,128)(2,1)} async-done(((bf16[256,2048]{1,0:T(8,128)(2,1)}), bf16[2048,2048]{1,0:T(8,128)(2,1)}) %all-gather.17.cloned.1.call-update) | async-done | bytes 8388624 | tf_op jit(solution)/shard_map/all_gather | solution.py:234
  554.8 19.0 %fusion.95 = f32[2048,1536]{0,1:T(8,128)} fusion(bf16[2048,2048]{1,0:T(8,128)(2,1)} %all-gather.17.cloned.1.call-done, bf16[2048,2304]{0,1:T(8,128)(2,1)} %all-gather.19.cloned.1.call-done), kind=kOutput, calls=%fused_computation.134 | convolution fusion | flops 12884901888 | bytes 27262976 | tf_op jit(solution)/shard_map/dot_general | solution.py:237
  573.7 37.2 %all-gather.21.cloned.1.call-done = bf16[2048,2048]{1,0:T(8,128)(2,1)} async-done(((bf16[256,2048]{1,0:T(8,128)(2,1)}), bf16[2048,2048]{1,0:T(8,128)(2,1)}) %all-gather.21.cloned.1.call-update) | async-done | bytes 8388624 | tf_op jit(solution)/shard_map/all_gather | solution.py:192
  629.3 18.7 %convolution_convert_fusion.3 = bf16[2048,2048]{1,0:T(8,128)(2,1)} fusion(bf16[2048,2304]{0,1:T(8,128)(2,1)} %all-gather.19.cloned.1.call-done, bf16[2048,768]{0,1:T(8,128)(2,1)} %get-tuple-element.680, bf16[2048,768]{0,1:T(8,128)(2,1)S(1)} %get-tuple-element.679), kind=kOutput, calls=%fused_computation.117 | convolution fusion | flops 12901679104 | bytes 20971520 | tf_op jit(solution)/shard_map/dot_general | solution.py:51
  660.0 59.5 %reduce-scatter.9.cloned.1.call-done = bf16[256,2048]{1,0:T(8,128)(2,1)} async-done(((bf16[2048,2048]{1,0:T(8,128)(2,1)}), bf16[256,2048]{1,0:T(8,128)(2,1)}) %reduce-scatter.9.cloned.1.call-update) | async-done | bytes 1048592 | tf_op jit(solution)/shard_map/reduce_scatter | solution.py:249
  722.5 72.2 %reduce-scatter.7.cloned.1.call-done = bf16[256,2048]{1,0:T(8,128)(2,1)} async-done(((bf16[2048,2048]{1,0:T(8,128)(2,1)}), bf16[256,2048]{1,0:T(8,128)(2,1)}) %reduce-scatter.7.cloned.1.call-update) | async-done | bytes 1048592 | tf_op jit(solution)/shard_map/reduce_scatter | solution.py:261
  811.1 25.8 %all-to-all-done.2 = bf16[256,4,512]{2,0,1:T(8,128)(2,1)} async-done(((bf16[256,4,512]{2,0,1:T(8,128)(2,1)}), bf16[256,4,512]{2,0,1:T(8,128)(2,1)}, u32[]{:S(2)}, u32[]{:S(2)}) %all-to-all-start.2) | async-done | bytes 1048608 | tf_op jit(solution)/shard_map/all_to_all | solution.py:279
  839.5 123.5 %while.37 = (s32[]{:T(128)}, f32[1024,128]{1,0:T(8,128)}, f32[1024,128]{1,0:T(8,128)}, f32[2,512,4,128]{3,1,0,2:T(8,128)}, s32[2,512]{1,0:T(2,128)S(1)}, /*index...) while((s32[]{:T(128)}, f32[1024,128]{1,0:T(8,128)}, ...), condition=%wide.region_11.12_spmd.clone.clone, body=%wide.region_9.11_spmd.clone.clone.sunk | while | flops 2742048256 | bytes 106783928 | solution.py:128
  850.3 22.8 %fusion.228 = f32[2,512,4,128]{3,1,0,2:T(8,128)} fusion(f32[2,512,4,128]{3,1,0,2:T(8,128)} %get-tuple-element.900, s32[]{:T(128)} %get-tuple-element.897, f32[512,4,1024]{2,0,1:T(8,128)} %fusion.223, f32[512,4,1024]{2,0,1:T(8,128)} %fusion.224, f32[4,512]{1,0:T(4,128)S(1)} %dynamic-slice_bitcast_fusion.2, pred[512,1024]{1,0:T(8,128)(4,1)} %fusion.225, ...), kind=kOutput, calls=%fused_computation.67.clone.1 | convolution fusion | flops 559942656 | bytes 35930624 | tf_op jit(solution)/shard_map/while/body/eval_jaxpr/hqk,kd->qhd/dot_general | solution.py:113
  873.1 21.3 %fusion.226 = f32[1024,128]{1,0:T(8,128)} fusion(f32[512,4,1024]{2,0,1:T(8,128)} %fusion.223, f32[512,4,1024]{2,0,1:T(8,128)} %fusion.224, f32[4,512]{1,0:T(4,128)S(1)} %dynamic-slice_bitcast_fusion.2, pred[512,1024]{1,0:T(8,128)(4,1)} %fusion.225, f32[1024,128]{1,0:T(8,128)} %get-tuple-element.898, ...), kind=kOutput, calls=%fused_computation.70.clone.1 | convolution fusion | flops 560204800 | bytes 36192768 | tf_op jit(solution)/shard_map/while/body/eval_jaxpr/hqk,qhd->kd/dot_general | solution.py:116
  912.0 22.8 %fusion.228 = f32[2,512,4,128]{3,1,0,2:T(8,128)} fusion(f32[2,512,4,128]{3,1,0,2:T(8,128)} %get-tuple-element.900, s32[]{:T(128)} %get-tuple-element.897, f32[512,4,1024]{2,0,1:T(8,128)} %fusion.223, f32[512,4,1024]{2,0,1:T(8,128)} %fusion.224, f32[4,512]{1,0:T(4,128)S(1)} %dynamic-slice_bitcast_fusion.2, pred[512,1024]{1,0:T(8,128)(4,1)} %fusion.225, ...), kind=kOutput, calls=%fused_computation.67.clone.1 | convolution fusion | flops 559942656 | bytes 35930624 | tf_op jit(solution)/shard_map/while/body/eval_jaxpr/hqk,kd->qhd/dot_general | solution.py:113
  934.8 21.3 %fusion.226 = f32[1024,128]{1,0:T(8,128)} fusion(f32[512,4,1024]{2,0,1:T(8,128)} %fusion.223, f32[512,4,1024]{2,0,1:T(8,128)} %fusion.224, f32[4,512]{1,0:T(4,128)S(1)} %dynamic-slice_bitcast_fusion.2, pred[512,1024]{1,0:T(8,128)(4,1)} %fusion.225, f32[1024,128]{1,0:T(8,128)} %get-tuple-element.898, ...), kind=kOutput, calls=%fused_computation.70.clone.1 | convolution fusion | flops 560204800 | bytes 36192768 | tf_op jit(solution)/shard_map/while/body/eval_jaxpr/hqk,qhd->kd/dot_general | solution.py:116
  977.2 41.2 %all_to_all.62 = bf16[4,256,512]{2,1,0:T(8,128)(2,1)} all-to-all(bf16[4,256,512]{2,1,0:T(8,128)(2,1)} %convert_element_type.151), channel_id=1, replica_groups=mesh['grp'=8,'seq'=4] {'seq'}, dimensions={0} | all-to-all | bytes 2097152 | tf_op jit(solution)/shard_map/all_to_all | solution.py:306
  1090.2 79.3 %reduce-scatter.13.cloned.1.call-done = bf16[64,2304]{1,0:T(8,128)(2,1)} async-done(((bf16[2048,2304]{1,0:T(8,128)(2,1)}), bf16[64,2304]{1,0:T(8,128)(2,1)}) %reduce-scatter.13.cloned.1.call-update) | async-done | bytes 294928 | tf_op jit(solution)/shard_map/reduce_scatter | solution.py:288
  1169.6 187.0 %reduce-scatter.15.cloned.1.call-done = bf16[64,2048]{1,0:T(8,128)(2,1)} async-done(((bf16[2048,2048]{1,0:T(8,128)(2,1)}), bf16[64,2048]{1,0:T(8,128)(2,1)}) %reduce-scatter.15.cloned.1.call-update) | async-done | bytes 262160 | tf_op jit(solution)/shard_map/reduce_scatter | solution.py:288
  1356.7 161.1 %reduce-scatter.17.cloned.1.call-done = bf16[512,2304]{0,1:T(8,128)(2,1)} async-done(((bf16[2048,2304]{0,1:T(8,128)(2,1)}), bf16[512,2304]{0,1:T(8,128)(2,1)}) %reduce-scatter.17.cloned.1.call-update) | async-done | bytes 2359312 | tf_op jit(solution)/shard_map/reduce_scatter | solution.py:258
  1534.5 41.6 %psum.7 = f32[2,2048]{1,0:T(2,128)S(1)} all-reduce(f32[2,2048]{1,0:T(2,128)S(1)} %pad_maximum_fusion.12), channel_id=1, replica_groups=mesh['grp'=8,'seq'=4] {'grp','seq'}, use_global_device_ids=true, to_apply=%region_20.21 | all-reduce | flops 4096 | bytes 32768 | tf_op jit(solution)/shard_map/psum | solution.py:322
  1605.0 76.1 %all-gather.27.cloned.1.call-done = bf16[144,512,128]{2,1,0:T(8,128)(2,1)} async-done(((bf16[18,512,128]{2,1,0:T(8,128)(2,1)}), bf16[144,512,128]{2,1,0:T(8,128)(2,1)}) %all-gather.27.cloned.1.call-update) | async-done | bytes 18874384 | tf_op jit(solution)/shard_map/all_gather | solution.py:260
  (243 shorter events, 390.7 us)
Async XLA Ops:
  7.2 1682.9 %copy-start = (f32[21,128,128]{2,1,0:T(8,128)S(1)}, f32[21,128,128]{2,1,0:T(8,128)}, u32[]{:S(2)}) copy-start(f32[21,128,128]{2,1,0:T(8,128)} %param.26) | copy-start | bytes 4128772
  7.2 117.5 %all-gather.11.cloned.1.call-start = ((), (), s32[]{:S(2)}) async-start(), calls=%async_computation.10 | async-start | bytes 24772608 | tf_op jit(solution)/shard_map/all_gather | solution.py:172
  7.9 174.9 %all-gather.13.cloned.1.call-start = ((), (), s32[]{:S(2)}) async-start(), calls=%async_computation.11 | async-start | bytes 2785280 | tf_op jit(solution)/shard_map/all_gather | solution.py:183
  8.7 174.4 %copy-start.1 = (s32[166]{0:T(256)S(1)}, s32[166]{0:T(256)}, u32[]{:S(2)}) copy-start(s32[166]{0:T(256)} %param.20) | copy-start | bytes 1996
  8.7 175.3 %copy-start.7 = (bf16[256,2048]{1,0:T(8,128)(2,1)S(1)}, bf16[256,2048]{1,0:T(8,128)(2,1)}, u32[]{:S(2)}) copy-start(bf16[256,2048]{1,0:T(8,128)(2,1)} %param.17) | copy-start | bytes 3145732
  134.4 143.5 %all-gather.15.cloned.1.call-start = ((), (), s32[]{:S(2)}) async-start(), calls=%async_computation.12 | async-start | bytes 20054016 | tf_op jit(solution)/shard_map/all_gather | solution.py:184
  182.9 317.0 %all-gather.19.cloned.1.call-start = ((), (), s32[]{:S(2)}) async-start(), calls=%async_computation.14 | async-start | bytes 11796480 | tf_op jit(solution)/shard_map/all_gather | solution.py:191
  202.7 136.5 %copy-start.22 = (f32[64]{0:T(128)}, f32[64]{0:T(128)S(1)}, u32[]{:S(2)}) copy-start(f32[64]{0:T(128)S(1)} %multiply_power_fusion) | copy-start | bytes 772
  291.7 91.5 %all-to-all-start = ((bf16[256,4,512]{0,2,1:T(8,128)(2,1)}), bf16[256,4,512]{0,2,1:T(8,128)(2,1)S(1)}, u32[]{:S(2)}, u32[]{:S(2)}) async-start(bf16[256,4,512]{0,2,1:T(8,128)(2,1)} %bitcast.5), calls=%async_computation | async-start | bytes 2097152 | tf_op jit(solution)/shard_map/all_to_all | solution.py:217
  296.3 258.4 %all-gather.17.cloned.1.call-start = ((), (), s32[]{:S(2)}) async-start(), calls=%async_computation.13 | async-start | bytes 9437184 | tf_op jit(solution)/shard_map/all_gather | solution.py:234
  481.1 129.9 %all-gather.21.cloned.1.call-start = ((), (), s32[]{:S(2)}) async-start(), calls=%async_computation.16 | async-start | bytes 9437184 | tf_op jit(solution)/shard_map/all_gather | solution.py:192
  481.7 237.9 %reduce-scatter.9.cloned.1.call-start = ((), (), s32[]{:S(2)}) async-start(), calls=%async_computation.17 | async-start | bytes 9437184 | tf_op jit(solution)/shard_map/reduce_scatter | solution.py:249
  648.1 146.6 %reduce-scatter.7.cloned.1.call-start = ((), (), s32[]{:S(2)}) async-start(), calls=%async_computation.15 | async-start | bytes 9437184 | tf_op jit(solution)/shard_map/reduce_scatter | solution.py:261
  806.5 30.4 %all-to-all-start.2 = ((bf16[256,4,512]{2,0,1:T(8,128)(2,1)}), bf16[256,4,512]{2,0,1:T(8,128)(2,1)}, u32[]{:S(2)}, u32[]{:S(2)}) async-start(bf16[256,4,512]{2,0,1:T(8,128)(2,1)} %bitcast.312), calls=%async_computation.4 | async-start | bytes 2097152 | tf_op jit(solution)/shard_map/all_to_all | solution.py:279
  811.1 208.7 %reduce-scatter.11.cloned.1.call-start = ((), (), s32[]{:S(2)}) async-start(), calls=%async_computation.18 | async-start | bytes 1310720 | tf_op jit(solution)/shard_map/reduce_scatter | solution.py:308
  839.5 127.7 %copy-start.23 = (f32[64]{0:T(128)S(1)}, f32[64]{0:T(128)}, u32[]{:S(2)}) copy-start(f32[64]{0:T(128)} %copy-done.22) | copy-start | bytes 772
  971.8 197.8 %reduce-scatter.13.cloned.1.call-start = ((), (), s32[]{:S(2)}) async-start(), calls=%async_computation.19 | async-start | bytes 9732096 | tf_op jit(solution)/shard_map/reduce_scatter | solution.py:288
  1034.7 321.9 %reduce-scatter.15.cloned.1.call-start = ((), (), s32[]{:S(2)}) async-start(), calls=%async_computation.21 | async-start | bytes 8650752 | tf_op jit(solution)/shard_map/reduce_scatter | solution.py:288
  1051.9 465.9 %reduce-scatter.17.cloned.1.call-start = ((), (), s32[]{:S(2)}) async-start(), calls=%async_computation.23 | async-start | bytes 11796480 | tf_op jit(solution)/shard_map/reduce_scatter | solution.py:258
  1090.1 432.0 %copy-start.2 = (s32[166]{0:T(256)S(1)}, s32[166]{0:T(256)}, u32[]{:S(2)}) copy-start(s32[166]{0:T(256)} %param.20) | copy-start | bytes 1996
  1090.2 491.9 %all-gather.23.cloned.1.call-start = ((), (), s32[]{:S(2)}) async-start(), calls=%async_computation.20 | async-start | bytes 2654208 | tf_op jit(solution)/shard_map/all_gather | solution.py:289
  1169.5 412.5 %all-gather.25.cloned.1.call-start = ((), (), s32[]{:S(2)}) async-start(), calls=%async_computation.22 | async-start | bytes 2359296 | tf_op jit(solution)/shard_map/all_gather | solution.py:289
  1356.6 324.5 %all-gather.27.cloned.1.call-start = ((), (), s32[]{:S(2)}) async-start(), calls=%async_computation.24 | async-start | bytes 21233664 | tf_op jit(solution)/shard_map/all_gather | solution.py:260
  1600.1 90.0 %copy-start.25 = (pred[21]{0:T(512)(128)(4,1)S(1)}, pred[21]{0:T(512)(128)(4,1)}, u32[]{:S(2)}) copy-start(pred[21]{0:T(512)(128)(4,1)} %broadcast_compare_fusion) | copy-start | bytes 67
  (23 other events, 592.1 us)
Sparse Core Ops, SparseCore 0:
  9.9 114.7 all-gather.10
  134.5 48.3 all-gather.12
  184.8 93.1 all-gather.14
  279.9 219.8 all-gather.18
  502.1 52.5 all-gather.16
  556.5 54.3 all-gather.20
  648.2 71.2 reduce-scatter.8
  723.4 71.2 reduce-scatter.6
  971.9 35.7 reduce-scatter.10
  1034.8 134.6 reduce-scatter.12
  1171.8 184.7 reduce-scatter.14
  1358.8 158.9 reduce-scatter.16
  1519.7 30.3 all-gather.22
  1551.9 28.3 all-gather.24
  1582.5 98.5 all-gather.26
where the time goes:
time: 1740 us; the launch traced here: 1730 us
  waiting for transfers between devices  1010 us (58%)
  matrix products  299 us (17%)
  blocking collectives  226 us (13%)
  local copies, waits for them, and re-layouts  112 us (6%)
  other arithmetic  59.6 us (3%)
    reduce_scatter x2, waiting for transfers between devices, reduce_rows(): lax.psum_scatter(blocks, ('grp', 'seq'), scatter_dimension=0, tiled=True)  266 us
    reduce_scatter x1, waiting for transfers between devices, local(): lax.psum_scatter(feed_grads, 'seq', scatter_dimension=0, tiled=True)  161 us
    all_gather x1, waiting for transfers between devices, local(): plane_tiles = lax.all_gather(weights_low, 'grp', axis=0, tiled=True)  116 us
    all_gather x1, waiting for transfers between devices, local(): feed_grads = lax.all_gather(feed_grads, 'grp', axis=0, tiled=True)  76.1 us
    all_gather x1, waiting for transfers between devices, local(): lax.all_gather(attn_weights, 'grp', axis=1, tiled=True)  73.6 us
    reduce_scatter x1, waiting for transfers between devices, local(): lax.psum_scatter(times_transpose(activated, down_weights).astype(jnp.bflo...  72.2 us
    reduce_scatter x1, waiting for transfers between devices, local(): lax.psum_scatter(times_transpose(gating_grad, gating_weights).astype(jnp....  59.5 us
    all_to_all x1, blocking collectives, local(): lax.all_to_all(head_context.reshape(-1, heads_here * HD).astype(jnp.bfloa...  59.3 us
  transfers between devices with their start and end apart: 17, of which 13 were waited for; matrix products, arithmetic and copies ran while one was open for 12% of the time, Pallas kernels for 0%

commit v1 on v0

--- a/solution.py
+++ b/solution.py
@@ -2,6 +2,7 @@
 import jax.numpy as jnp
 from jax import lax
 from jax.sharding import PartitionSpec as P
+from jax.lax import psum
 
 MODEL_WIDTH = 2048
 NH = 16
@@ -319,7 +320,9 @@
         * inverse_one**3
         * jnp.mean(tok_float * gains[0] * norm_one_grad, axis=-1, keepdims=True)
     )
-    gain_grads = lax.psum(jnp.stack([gain_one_term, gain_two_term]), ("grp", "seq"))
+    gain_grads = jnp.stack([gain_one_term, gain_two_term])
+    for j0 in ("seq", "grp"):
+        gain_grads = psum(gain_grads, j0)
     tile_count = tile_owner_slots.shape[0]
     tile_of_slot = (
         jnp.full((grp_count * slots_here,), tile_count, jnp.int32)

time: 1740 us -> 1740 us (level)
    psum x1 -> x2, blocking collectives: 41.6 us -> 41.2 us  [local(): gain_grads = psum(gain_grads, j0)]
where the time goes in v1:
time: 1740 us; the launch traced here: 1730 us
  waiting for transfers between devices  1010 us (58%)
  matrix products  299 us (17%)
  blocking collectives  226 us (13%)
  local copies, waits for them, and re-layouts  111 us (6%)
  other arithmetic  59.5 us (3%)
    reduce_scatter x2, waiting for transfers between devices, reduce_rows(): lax.psum_scatter(blocks, ('grp', 'seq'), scatter_dimension=0, tiled=True)  266 us
    reduce_scatter x1, waiting for transfers between devices, local(): lax.psum_scatter(feed_grads, 'seq', scatter_dimension=0, tiled=True)  161 us
    all_gather x1, waiting for transfers between devices, local(): plane_tiles = lax.all_gather(weights_low, 'grp', axis=0, tiled=True)  116 us
    all_gather x1, waiting for transfers between devices, local(): feed_grads = lax.all_gather(feed_grads, 'grp', axis=0, tiled=True)  75.8 us
    all_gather x1, waiting for transfers between devices, local(): lax.all_gather(attn_weights, 'grp', axis=1, tiled=True)  73.6 us
    reduce_scatter x1, waiting for transfers between devices, local(): lax.psum_scatter(times_transpose(activated, down_weights).astype(jnp.bflo...  72.2 us
    reduce_scatter x1, waiting for transfers between devices, local(): lax.psum_scatter(times_transpose(gating_grad, gating_weights).astype(jnp....  59.5 us
    all_to_all x1, blocking collectives, local(): lax.all_to_all(head_context.reshape(-1, heads_here * HD).astype(jnp.bfloa...  59.3 us
  transfers between devices with their start and end apart: 17, of which 13 were waited for; matrix products, arithmetic and copies ran while one was open for 12% of the time, Pallas kernels for 0%

profile of v1, /device:TPU:0, one launch (start us, length us, event | category | flops | bytes accessed | tf_op | source)
XLA Modules:
  0.0 1730.9 jit_solution(2232771411483398638)
XLA Ops:
  8.7 116.0 %all-gather.11.cloned.1.call-done = bf16[168,512,128]{2,1,0:T(8,128)(2,1)} async-done(((bf16[21,512,128]{2,1,0:T(8,128)(2,1)}), bf16[168,512,128]{2,1,0:T(8,128)(2,1)}) %all-gather.11.cloned.1.call-update) | async-done | bytes 22020112 | tf_op jit(solution)/shard_map/all_gather | solution.py:173
  134.4 48.4 %all-gather.13.cloned.1.call-done = bf16[4,64,4352]{2,1,0:T(8,128)(2,1)} async-done(((bf16[1,64,4352]{2,1,0:T(8,128)(2,1)}), bf16[4,64,4352]{2,1,0:T(8,128)(2,1)}) %all-gather.13.cloned.1.call-update) | async-done | bytes 2228240 | tf_op jit(solution)/shard_map/all_gather | solution.py:184
  204.3 73.6 %all-gather.15.cloned.1.call-done = bf16[4,512,4352]{2,1,0:T(8,128)(2,1)} async-done(((bf16[4,64,4352]{2,1,0:T(8,128)(2,1)}), bf16[4,512,4352]{2,1,0:T(8,128)(2,1)}) %all-gather.15.cloned.1.call-update) | async-done | bytes 17825808 | tf_op jit(solution)/shard_map/all_gather | solution.py:185
  296.3 40.8 %all-gather = s32[4,1,256]{2,1,0:T(1,128)S(1)} all-gather(s32[1,1,256]{2,1,0:T(1,128)} %bitcast.336), channel_id=1, replica_groups=mesh['grp'=8,'seq'=4] {'seq'}, dimensions={0}, use_global_device_ids=true | all-gather | bytes 5120 | tf_op jit(solution)/shard_map/all_gather | solution.py:214
  339.6 43.2 %all_gather.37 = bf16[1024,256]{0,1:T(8,128)(2,1)S(1)} all-gather(bf16[256,256]{0,1:T(8,128)(2,1)S(1)} %pad_maximum_fusion.11), channel_id=1, replica_groups=mesh['grp'=8,'seq'=4] {'seq'}, dimensions={0}, use_global_device_ids=true | all-gather | bytes 655360 | tf_op jit(solution)/shard_map/all_gather | solution.py:209
  410.6 59.3 %all_to_all.61 = bf16[4,256,512]{2,1,0:T(8,128)(2,1)} all-to-all(bf16[4,256,512]{2,1,0:T(8,128)(2,1)} %convert_element_type.137), channel_id=1, replica_groups=mesh['grp'=8,'seq'=4] {'seq'}, dimensions={0} | all-to-all | bytes 2097152 | tf_op jit(solution)/shard_map/all_to_all | solution.py:224
  499.8 54.9 %all-gather.17.cloned.1.call-done = bf16[2048,2048]{1,0:T(8,128)(2,1)} async-done(((bf16[256,2048]{1,0:T(8,128)(2,1)}), bf16[2048,2048]{1,0:T(8,128)(2,1)}) %all-gather.17.cloned.1.call-update) | async-done | bytes 8388624 | tf_op jit(solution)/shard_map/all_gather | solution.py:235
  554.8 19.1 %fusion.95 = f32[2048,1536]{0,1:T(8,128)} fusion(bf16[2048,2048]{1,0:T(8,128)(2,1)} %all-gather.17.cloned.1.call-done, bf16[2048,2304]{0,1:T(8,128)(2,1)} %all-gather.19.cloned.1.call-done), kind=kOutput, calls=%fused_computation.134 | convolution fusion | flops 12884901888 | bytes 27262976 | tf_op jit(solution)/shard_map/dot_general | solution.py:238
  573.8 37.1 %all-gather.21.cloned.1.call-done = bf16[2048,2048]{1,0:T(8,128)(2,1)} async-done(((bf16[256,2048]{1,0:T(8,128)(2,1)}), bf16[2048,2048]{1,0:T(8,128)(2,1)}) %all-gather.21.cloned.1.call-update) | async-done | bytes 8388624 | tf_op jit(solution)/shard_map/all_gather | solution.py:193
  629.3 18.7 %convolution_convert_fusion.3 = bf16[2048,2048]{1,0:T(8,128)(2,1)} fusion(bf16[2048,2304]{0,1:T(8,128)(2,1)} %all-gather.19.cloned.1.call-done, bf16[2048,768]{0,1:T(8,128)(2,1)} %get-tuple-element.680, bf16[2048,768]{0,1:T(8,128)(2,1)S(1)} %get-tuple-element.679), kind=kOutput, calls=%fused_computation.117 | convolution fusion | flops 12901679104 | bytes 20971520 | tf_op jit(solution)/shard_map/dot_general | solution.py:52
  660.0 59.5 %reduce-scatter.9.cloned.1.call-done = bf16[256,2048]{1,0:T(8,128)(2,1)} async-done(((bf16[2048,2048]{1,0:T(8,128)(2,1)}), bf16[256,2048]{1,0:T(8,128)(2,1)}) %reduce-scatter.9.cloned.1.call-update) | async-done | bytes 1048592 | tf_op jit(solution)/shard_map/reduce_scatter | solution.py:250
  722.5 72.2 %reduce-scatter.7.cloned.1.call-done = bf16[256,2048]{1,0:T(8,128)(2,1)} async-done(((bf16[2048,2048]{1,0:T(8,128)(2,1)}), bf16[256,2048]{1,0:T(8,128)(2,1)}) %reduce-scatter.7.cloned.1.call-update) | async-done | bytes 1048592 | tf_op jit(solution)/shard_map/reduce_scatter | solution.py:262
  811.1 25.8 %all-to-all-done.2 = bf16[256,4,512]{2,0,1:T(8,128)(2,1)} async-done(((bf16[256,4,512]{2,0,1:T(8,128)(2,1)}), bf16[256,4,512]{2,0,1:T(8,128)(2,1)}, u32[]{:S(2)}, u32[]{:S(2)}) %all-to-all-start.2) | async-done | bytes 1048608 | tf_op jit(solution)/shard_map/all_to_all | solution.py:280
  839.5 123.6 %while.37 = (s32[]{:T(128)}, f32[1024,128]{1,0:T(8,128)}, f32[1024,128]{1,0:T(8,128)}, f32[2,512,4,128]{3,1,0,2:T(8,128)}, s32[2,512]{1,0:T(2,128)S(1)}, /*index...) while((s32[]{:T(128)}, f32[1024,128]{1,0:T(8,128)}, ...), condition=%wide.region_11.12_spmd.clone.clone, body=%wide.region_9.11_spmd.clone.clone.sunk | while | flops 2742048256 | bytes 106783928 | solution.py:129
  850.3 22.9 %fusion.228 = f32[2,512,4,128]{3,1,0,2:T(8,128)} fusion(f32[2,512,4,128]{3,1,0,2:T(8,128)} %get-tuple-element.900, s32[]{:T(128)} %get-tuple-element.897, f32[512,4,1024]{2,0,1:T(8,128)} %fusion.223, f32[512,4,1024]{2,0,1:T(8,128)} %fusion.224, f32[4,512]{1,0:T(4,128)S(1)} %dynamic-slice_bitcast_fusion.2, pred[512,1024]{1,0:T(8,128)(4,1)} %fusion.225, ...), kind=kOutput, calls=%fused_computation.67.clone.1 | convolution fusion | flops 559942656 | bytes 35930624 | tf_op jit(solution)/shard_map/while/body/eval_jaxpr/hqk,kd->qhd/dot_general | solution.py:114
  873.2 21.2 %fusion.226 = f32[1024,128]{1,0:T(8,128)} fusion(f32[512,4,1024]{2,0,1:T(8,128)} %fusion.223, f32[512,4,1024]{2,0,1:T(8,128)} %fusion.224, f32[4,512]{1,0:T(4,128)S(1)} %dynamic-slice_bitcast_fusion.2, pred[512,1024]{1,0:T(8,128)(4,1)} %fusion.225, f32[1024,128]{1,0:T(8,128)} %get-tuple-element.898, ...), kind=kOutput, calls=%fused_computation.70.clone.1 | convolution fusion | flops 560204800 | bytes 36192768 | tf_op jit(solution)/shard_map/while/body/eval_jaxpr/hqk,qhd->kd/dot_general | solution.py:117
  912.0 22.9 %fusion.228 = f32[2,512,4,128]{3,1,0,2:T(8,128)} fusion(f32[2,512,4,128]{3,1,0,2:T(8,128)} %get-tuple-element.900, s32[]{:T(128)} %get-tuple-element.897, f32[512,4,1024]{2,0,1:T(8,128)} %fusion.223, f32[512,4,1024]{2,0,1:T(8,128)} %fusion.224, f32[4,512]{1,0:T(4,128)S(1)} %dynamic-slice_bitcast_fusion.2, pred[512,1024]{1,0:T(8,128)(4,1)} %fusion.225, ...), kind=kOutput, calls=%fused_computation.67.clone.1 | convolution fusion | flops 559942656 | bytes 35930624 | tf_op jit(solution)/shard_map/while/body/eval_jaxpr/hqk,kd->qhd/dot_general | solution.py:114
  934.9 21.3 %fusion.226 = f32[1024,128]{1,0:T(8,128)} fusion(f32[512,4,1024]{2,0,1:T(8,128)} %fusion.223, f32[512,4,1024]{2,0,1:T(8,128)} %fusion.224, f32[4,512]{1,0:T(4,128)S(1)} %dynamic-slice_bitcast_fusion.2, pred[512,1024]{1,0:T(8,128)(4,1)} %fusion.225, f32[1024,128]{1,0:T(8,128)} %get-tuple-element.898, ...), kind=kOutput, calls=%fused_computation.70.clone.1 | convolution fusion | flops 560204800 | bytes 36192768 | tf_op jit(solution)/shard_map/while/body/eval_jaxpr/hqk,qhd->kd/dot_general | solution.py:117
  977.2 41.2 %all_to_all.62 = bf16[4,256,512]{2,1,0:T(8,128)(2,1)} all-to-all(bf16[4,256,512]{2,1,0:T(8,128)(2,1)} %convert_element_type.151), channel_id=1, replica_groups=mesh['grp'=8,'seq'=4] {'seq'}, dimensions={0} | all-to-all | bytes 2097152 | tf_op jit(solution)/shard_map/all_to_all | solution.py:307
  1090.2 79.0 %reduce-scatter.13.cloned.1.call-done = bf16[64,2304]{1,0:T(8,128)(2,1)} async-done(((bf16[2048,2304]{1,0:T(8,128)(2,1)}), bf16[64,2304]{1,0:T(8,128)(2,1)}) %reduce-scatter.13.cloned.1.call-update) | async-done | bytes 294928 | tf_op jit(solution)/shard_map/reduce_scatter | solution.py:289
  1169.3 187.3 %reduce-scatter.15.cloned.1.call-done = bf16[64,2048]{1,0:T(8,128)(2,1)} async-done(((bf16[2048,2048]{1,0:T(8,128)(2,1)}), bf16[64,2048]{1,0:T(8,128)(2,1)}) %reduce-scatter.15.cloned.1.call-update) | async-done | bytes 262160 | tf_op jit(solution)/shard_map/reduce_scatter | solution.py:289
  1356.7 161.1 %reduce-scatter.17.cloned.1.call-done = bf16[512,2304]{0,1:T(8,128)(2,1)} async-done(((bf16[2048,2304]{0,1:T(8,128)(2,1)}), bf16[512,2304]{0,1:T(8,128)(2,1)}) %reduce-scatter.17.cloned.1.call-update) | async-done | bytes 2359312 | tf_op jit(solution)/shard_map/reduce_scatter | solution.py:259
  1552.6 23.0 %psum.15 = f32[2,2048]{1,0:T(2,128)S(1)} all-reduce(f32[2,2048]{1,0:T(2,128)S(1)} %psum.14), channel_id=1, replica_groups=mesh['grp'=8,'seq'=4] {'grp'}, use_global_device_ids=true, to_apply=%region_21.22 | all-reduce | flops 4096 | bytes 32768 | tf_op jit(solution)/shard_map/psum | solution.py:325
  1604.5 75.8 %all-gather.27.cloned.1.call-done = bf16[144,512,128]{2,1,0:T(8,128)(2,1)} async-done(((bf16[18,512,128]{2,1,0:T(8,128)(2,1)}), bf16[144,512,128]{2,1,0:T(8,128)(2,1)}) %all-gather.27.cloned.1.call-update) | async-done | bytes 18874384 | tf_op jit(solution)/shard_map/all_gather | solution.py:261
  (244 shorter events, 408.8 us)
Async XLA Ops:
  7.2 1682.1 %copy-start = (f32[21,128,128]{2,1,0:T(8,128)S(1)}, f32[21,128,128]{2,1,0:T(8,128)}, u32[]{:S(2)}) copy-start(f32[21,128,128]{2,1,0:T(8,128)} %param.26) | copy-start | bytes 4128772
  7.2 117.5 %all-gather.11.cloned.1.call-start = ((), (), s32[]{:S(2)}) async-start(), calls=%async_computation.10 | async-start | bytes 24772608 | tf_op jit(solution)/shard_map/all_gather | solution.py:173
  7.9 174.9 %all-gather.13.cloned.1.call-start = ((), (), s32[]{:S(2)}) async-start(), calls=%async_computation.11 | async-start | bytes 2785280 | tf_op jit(solution)/shard_map/all_gather | solution.py:184
  8.7 174.4 %copy-start.1 = (s32[166]{0:T(256)S(1)}, s32[166]{0:T(256)}, u32[]{:S(2)}) copy-start(s32[166]{0:T(256)} %param.20) | copy-start | bytes 1996
  8.7 175.3 %copy-start.7 = (bf16[256,2048]{1,0:T(8,128)(2,1)S(1)}, bf16[256,2048]{1,0:T(8,128)(2,1)}, u32[]{:S(2)}) copy-start(bf16[256,2048]{1,0:T(8,128)(2,1)} %param.17) | copy-start | bytes 3145732
  134.4 143.5 %all-gather.15.cloned.1.call-start = ((), (), s32[]{:S(2)}) async-start(), calls=%async_computation.12 | async-start | bytes 20054016 | tf_op jit(solution)/shard_map/all_gather | solution.py:185
  182.9 317.0 %all-gather.19.cloned.1.call-start = ((), (), s32[]{:S(2)}) async-start(), calls=%async_computation.14 | async-start | bytes 11796480 | tf_op jit(solution)/shard_map/all_gather | solution.py:192
  202.7 136.5 %copy-start.22 = (f32[64]{0:T(128)}, f32[64]{0:T(128)S(1)}, u32[]{:S(2)}) copy-start(f32[64]{0:T(128)S(1)} %multiply_power_fusion) | copy-start | bytes 772
  291.7 91.5 %all-to-all-start = ((bf16[256,4,512]{0,2,1:T(8,128)(2,1)}), bf16[256,4,512]{0,2,1:T(8,128)(2,1)S(1)}, u32[]{:S(2)}, u32[]{:S(2)}) async-start(bf16[256,4,512]{0,2,1:T(8,128)(2,1)} %bitcast.5), calls=%async_computation | async-start | bytes 2097152 | tf_op jit(solution)/shard_map/all_to_all | solution.py:218
  296.3 258.4 %all-gather.17.cloned.1.call-start = ((), (), s32[]{:S(2)}) async-start(), calls=%async_computation.13 | async-start | bytes 9437184 | tf_op jit(solution)/shard_map/all_gather | solution.py:235
  481.2 129.7 %all-gather.21.cloned.1.call-start = ((), (), s32[]{:S(2)}) async-start(), calls=%async_computation.16 | async-start | bytes 9437184 | tf_op jit(solution)/shard_map/all_gather | solution.py:193
  481.8 237.7 %reduce-scatter.9.cloned.1.call-start = ((), (), s32[]{:S(2)}) async-start(), calls=%async_computation.17 | async-start | bytes 9437184 | tf_op jit(solution)/shard_map/reduce_scatter | solution.py:250
  648.0 146.6 %reduce-scatter.7.cloned.1.call-start = ((), (), s32[]{:S(2)}) async-start(), calls=%async_computation.15 | async-start | bytes 9437184 | tf_op jit(solution)/shard_map/reduce_scatter | solution.py:262
  806.5 30.4 %all-to-all-start.2 = ((bf16[256,4,512]{2,0,1:T(8,128)(2,1)}), bf16[256,4,512]{2,0,1:T(8,128)(2,1)}, u32[]{:S(2)}, u32[]{:S(2)}) async-start(bf16[256,4,512]{2,0,1:T(8,128)(2,1)} %bitcast.312), calls=%async_computation.4 | async-start | bytes 2097152 | tf_op jit(solution)/shard_map/all_to_all | solution.py:280
  811.1 208.8 %reduce-scatter.11.cloned.1.call-start = ((), (), s32[]{:S(2)}) async-start(), calls=%async_computation.18 | async-start | bytes 1310720 | tf_op jit(solution)/shard_map/reduce_scatter | solution.py:309
  839.5 127.8 %copy-start.23 = (f32[64]{0:T(128)S(1)}, f32[64]{0:T(128)}, u32[]{:S(2)}) copy-start(f32[64]{0:T(128)} %copy-done.22) | copy-start | bytes 772
  971.8 197.4 %reduce-scatter.13.cloned.1.call-start = ((), (), s32[]{:S(2)}) async-start(), calls=%async_computation.19 | async-start | bytes 9732096 | tf_op jit(solution)/shard_map/reduce_scatter | solution.py:289
  1034.7 321.9 %reduce-scatter.15.cloned.1.call-start = ((), (), s32[]{:S(2)}) async-start(), calls=%async_computation.21 | async-start | bytes 8650752 | tf_op jit(solution)/shard_map/reduce_scatter | solution.py:289
  1051.9 465.9 %reduce-scatter.17.cloned.1.call-start = ((), (), s32[]{:S(2)}) async-start(), calls=%async_computation.23 | async-start | bytes 11796480 | tf_op jit(solution)/shard_map/reduce_scatter | solution.py:259
  1090.2 431.9 %copy-start.2 = (s32[166]{0:T(256)S(1)}, s32[166]{0:T(256)}, u32[]{:S(2)}) copy-start(s32[166]{0:T(256)} %param.20) | copy-start | bytes 1996
  1090.2 491.4 %all-gather.23.cloned.1.call-start = ((), (), s32[]{:S(2)}) async-start(), calls=%async_computation.20 | async-start | bytes 2654208 | tf_op jit(solution)/shard_map/all_gather | solution.py:290
  1169.2 412.3 %all-gather.25.cloned.1.call-start = ((), (), s32[]{:S(2)}) async-start(), calls=%async_computation.22 | async-start | bytes 2359296 | tf_op jit(solution)/shard_map/all_gather | solution.py:290
  1356.6 323.7 %all-gather.27.cloned.1.call-start = ((), (), s32[]{:S(2)}) async-start(), calls=%async_computation.24 | async-start | bytes 21233664 | tf_op jit(solution)/shard_map/all_gather | solution.py:261
  1599.6 89.7 %copy-start.25 = (pred[21]{0:T(512)(128)(4,1)S(1)}, pred[21]{0:T(512)(128)(4,1)}, u32[]{:S(2)}) copy-start(pred[21]{0:T(512)(128)(4,1)} %broadcast_compare_fusion) | copy-start | bytes 67
  (23 other events, 591.1 us)
Sparse Core Ops, SparseCore 0:
  9.9 114.7 all-gather.10
  134.5 48.3 all-gather.12
  184.8 93.1 all-gather.14
  279.9 219.8 all-gather.18
  502.1 52.5 all-gather.16
  556.5 54.3 all-gather.20
  648.2 71.2 reduce-scatter.8
  723.3 71.2 reduce-scatter.6
  971.9 35.7 reduce-scatter.10
  1034.8 134.3 reduce-scatter.12
  1171.5 185.0 reduce-scatter.14
  1358.8 158.9 reduce-scatter.16
  1519.7 29.8 all-gather.22
  1551.3 27.9 all-gather.24
  1581.6 98.6 all-gather.26
